TPU v7x, 512 devices: a whole 4x4x16 slice. The times are simulated.
512 devices in a mesh: blk: 32 (over y_lo, z), gy: 4 (over x), rep: 4 (over y_hi, core).
Axes of the slice: x: 4, y: 4 (y_hi: 2, y_lo: 2; y = y_hi * 2 + y_lo), z: 16, core: 2. Of those that a mesh axis runs over, the one named last changes fastest.
Arguments:
- grain_id: int32 [128, 32, 512], P('blk', 'gy', 'rep'), may hold values from 0 to 255
- init_masks: int32 [2, 128, 32, 512], P(None, 'blk', 'gy', 'rep'), may hold values from 0 to 1, as said below
- target_masks: int32 [2, 128, 32, 512], P(None, 'blk', 'gy', 'rep'), may hold values from 0 to 1, as said below
- emb_table: bfloat16 [256, 8], replicated, may hold values from -6 to 6
- w_in: float32 [64, 10], P('rep'), may hold values from -2 to 2
- b_in: float32 [64], P('rep'), may hold values from -3 to 3
- w_mid: float32 [64, 64], P('rep'), may hold values from -0.75 to 0.75
- b_mid: float32 [64], P('rep'), may hold values from -3 to 3
- w_out: float32 [6, 64], P(None, 'rep'), may hold values from -0.75 to 0.75
- b_out: float32 [6], replicated, may hold values from -4 to 4
Outputs:
- final_state: float32 [2, 128, 32, 512], P(None, 'blk', 'gy', 'rep')
- loss: float32 [], replicated
- grad_w_in: float32 [64, 10], P('rep')
- grad_b_in: float32 [64], P('rep')
- grad_w_mid: float32 [64, 64], P('rep')
- grad_b_mid: float32 [64], P('rep')
- grad_w_out: float32 [6, 64], P(None, 'rep')
- grad_b_out: float32 [6], replicated
- start_sensitivity: float32 [2, 128, 32, 512], P(None, 'blk', 'gy', 'rep')
Inputs may be any that keep to these rules, and one draw needn't show every extreme that they name: `init_masks`: 0 or 1 in every cell. `target_masks`: 0 or 1 in every cell.
All inputs are finite; a program needn't handle non-finite values.
Results may differ from a plain program's by a relative error of at most 0.0054.
The roundings to bfloat16 on the way count: a program that leaves them out, or rounds other values in their place, can miss the bound.
Values may be sent and summed in bfloat16 or wider, within the bound.
A program may use at most 64 MiB of HBM per device.

v0:
```python
import jax
import jax.numpy as jnp
from jax import lax
from jax.sharding import PartitionSpec as P

STEPS = 4
RATE_MAX = 0.15
AXES = (("rep", 3), ("gy", 2), ("blk", 1))


def ring_perms(axis):
    count = lax.axis_size(axis)
    forward = [(i, (i + 1) % count) for i in range(count)]
    backward = [((i + 1) % count, i) for i in range(count)]
    return (forward, backward)


def exchange_faces(fields):
    faces = []
    for direction, (axis, dim) in enumerate(AXES):
        block = fields[direction]
        forward, backward = ring_perms(axis)
        size = block.shape[dim]
        low = lax.ppermute(lax.slice_in_dim(block, size - 1, size, axis=dim), axis, forward)
        high = lax.ppermute(lax.slice_in_dim(block, 0, 1, axis=dim), axis, backward)
        faces.append((low, high))
    return faces


def shifted(block, low, high, dim, offset):
    size = block.shape[dim]
    if offset == 1:
        return jnp.concatenate([lax.slice_in_dim(block, 1, size, axis=dim), high], axis=dim)
    return jnp.concatenate([low, lax.slice_in_dim(block, 0, size - 1, axis=dim)], axis=dim)


def diffuse(field, field_faces, rates, rate_faces):
    summed = field
    for direction, (axis, dim) in enumerate(AXES):
        rate_here = rates[direction::3]
        for offset in (1, -1):
            low, high = field_faces[direction]
            rlow, rhigh = rate_faces[direction]
            rate_next = shifted(rate_here, rlow, rhigh, dim, offset)
            summed = summed + 0.5 * (rate_here + rate_next) * (
                shifted(field, low, high, dim, offset) - field
            )
    return summed


def rate_cotangent(state, state_faces, adjoint, adjoint_faces):
    pieces_list = []
    for direction, (axis, dim) in enumerate(AXES):
        summed = jnp.zeros_like(state)
        for offset in (1, -1):
            slow, shigh = state_faces[direction]
            alow, ahigh = adjoint_faces[direction]
            summed = summed + (shifted(state, slow, shigh, dim, offset) - state) * (
                shifted(adjoint, alow, ahigh, dim, offset) - adjoint
            )
        pieces_list.append(-0.5 * summed)
    stacked = jnp.stack(pieces_list, axis=1)
    return stacked.reshape((6,) + stacked.shape[2:])


def embed_lookup(emb_table, grain_flat):
    table_rows = emb_table.shape[0]
    one_hot = (grain_flat[None, :] == lax.broadcasted_iota(jnp.int32, (table_rows, 1), 0)).astype(
        jnp.bfloat16
    )
    looked = jnp.dot(emb_table.T, one_hot, preferred_element_type=jnp.float32)
    return looked.astype(jnp.bfloat16)


def forward_layers(params, features):
    w_in, b_in, w_mid, b_mid, w_out, b_out = params
    act_one = jnp.tanh(
        jnp.dot(w_in, features, preferred_element_type=jnp.float32)
        + b_in.astype(jnp.float32)[:, None]
    )
    hid_one = act_one.astype(jnp.bfloat16)
    act_two = jnp.tanh(
        jnp.dot(w_mid, hid_one, preferred_element_type=jnp.float32)
        + b_mid.astype(jnp.float32)[:, None]
    )
    hid_two = act_two.astype(jnp.bfloat16)
    logits = (
        jnp.dot(w_out, hid_two, preferred_element_type=jnp.float32)
        + b_out.astype(jnp.float32)[:, None]
    )
    return (RATE_MAX * jax.nn.sigmoid(logits), act_one, hid_one, act_two, hid_two)


def backward_layers(params, features, rate_grad, forward_values):
    w_in, b_in, w_mid, b_mid, w_out, b_out = params
    rate_values, act_one, hid_one, act_two, hid_two = forward_values
    out_grad = (rate_grad * rate_values * (1.0 - rate_values / RATE_MAX)).astype(jnp.bfloat16)
    two_grad = (
        jnp.dot(w_out.T, out_grad, preferred_element_type=jnp.float32) * (1.0 - act_two * act_two)
    ).astype(jnp.bfloat16)
    one_grad = (
        jnp.dot(w_mid.T, two_grad, preferred_element_type=jnp.float32) * (1.0 - act_one * act_one)
    ).astype(jnp.bfloat16)
    grad_terms = (
        jnp.dot(one_grad, features.T, preferred_element_type=jnp.float32),
        jnp.sum(one_grad, axis=1, dtype=jnp.float32),
        jnp.dot(two_grad, hid_one.T, preferred_element_type=jnp.float32),
        jnp.sum(two_grad, axis=1, dtype=jnp.float32),
        jnp.dot(out_grad, hid_two.T, preferred_element_type=jnp.float32),
        jnp.sum(out_grad, axis=1, dtype=jnp.float32),
    )
    state_grad = jnp.dot(w_in[:, -2:].T, one_grad, preferred_element_type=jnp.float32)
    return (grad_terms, state_grad)


def gather_params(w_in, b_in, w_mid, b_mid, w_out, b_out):
    n_in = w_in.shape[1]
    n_mid = w_mid.shape[1]
    packed = jnp.concatenate([w_in, b_in[:, None], w_mid, b_mid[:, None], w_out.T], axis=1).astype(
        jnp.bfloat16
    )
    full = lax.all_gather(packed, "rep", axis=0, tiled=True)
    col = 0
    w_in_b = full[:, col : col + n_in]
    col += n_in
    b_in_b = full[:, col]
    col += 1
    w_mid_b = full[:, col : col + n_mid]
    col += n_mid
    b_mid_b = full[:, col]
    col += 1
    w_out_b = full[:, col:].T
    return (w_in_b, b_in_b, w_mid_b, b_mid_b, w_out_b, b_out.astype(jnp.bfloat16))


def per_device(
    grain_id, init_masks, target_masks, emb_table, w_in, b_in, w_mid, b_mid, w_out, b_out
):
    params = gather_params(w_in, b_in, w_mid, b_mid, w_out, b_out)
    depth_cells, row_cells, col_cells = grain_id.shape
    cell_count = depth_cells * row_cells * col_cells
    block_shape = (depth_cells, row_cells, col_cells)
    embedding = embed_lookup(emb_table, grain_id.reshape(cell_count))
    state_now = init_masks.astype(jnp.float32)
    history = []
    for step_index in range(STEPS):
        features = jnp.concatenate(
            [embedding, state_now.reshape(2, cell_count).astype(jnp.bfloat16)], axis=0
        )
        rate_values = forward_layers(params, features)[0].reshape((6,) + block_shape)
        faces = exchange_faces(
            [jnp.concatenate([state_now, rate_values[d::3]], axis=0) for d in range(3)]
        )
        state_faces = [(low[:2], high[:2]) for low, high in faces]
        rate_faces = [(low[2:], high[2:]) for low, high in faces]
        history.append((state_now, state_faces, rate_values, rate_faces))
        state_now = diffuse(state_now, state_faces, rate_values, rate_faces)
    misfit = state_now - target_masks.astype(jnp.float32)
    total_cells = float(
        cell_count * lax.axis_size("blk") * lax.axis_size("gy") * lax.axis_size("rep")
    )
    loss_part = jnp.sum(misfit * misfit) / (4.0 * total_cells)
    adjoint = misfit / (2.0 * total_cells)
    grad_sums = None
    for step_index in reversed(range(STEPS)):
        state_t, state_faces, rate_values, rate_faces = history[step_index]
        adjoint_faces = exchange_faces([adjoint] * 3)
        rate_grad = rate_cotangent(state_t, state_faces, adjoint, adjoint_faces).reshape(
            6, cell_count
        )
        features = jnp.concatenate(
            [embedding, state_t.reshape(2, cell_count).astype(jnp.bfloat16)], axis=0
        )
        forward_values = forward_layers(params, features)
        step_terms, state_grad = backward_layers(params, features, rate_grad, forward_values)
        if grad_sums is None:
            grad_sums = step_terms
        else:
            grad_sums = tuple(
                (earlier + later_term for earlier, later_term in zip(grad_sums, step_terms))
            )
        adjoint = diffuse(adjoint, adjoint_faces, rate_values, rate_faces) + state_grad.reshape(
            (2,) + block_shape
        )
    start_sensitivity = adjoint * (2.0 * total_cells)
    pieces = list(grad_sums) + [loss_part[None]]
    flat = jnp.concatenate([piece.reshape(-1) for piece in pieces])
    summed_flat = lax.psum(flat, ("blk", "gy", "rep"))
    summed = []
    start = 0
    for piece in pieces:
        summed.append(summed_flat[start : start + piece.size].reshape(piece.shape))
        start += piece.size
    position = lax.axis_index("rep")
    share_width = w_in.shape[0]
    grad_w_in = lax.dynamic_slice_in_dim(summed[0], position * share_width, share_width, 0)
    grad_b_in = lax.dynamic_slice_in_dim(summed[1], position * share_width, share_width, 0)
    grad_w_mid = lax.dynamic_slice_in_dim(summed[2], position * share_width, share_width, 0)
    grad_b_mid = lax.dynamic_slice_in_dim(summed[3], position * share_width, share_width, 0)
    grad_w_out = lax.dynamic_slice_in_dim(summed[4], position * share_width, share_width, 1)
    grad_b_out = summed[5]
    loss_total = summed[6][0]
    return (
        state_now,
        loss_total,
        grad_w_in,
        grad_b_in,
        grad_w_mid,
        grad_b_mid,
        grad_w_out,
        grad_b_out,
        start_sensitivity,
    )


def solution(mesh):
    in_specs = (
        P("blk", "gy", "rep"),
        P(None, "blk", "gy", "rep"),
        P(None, "blk", "gy", "rep"),
        P(),
        P("rep", None),
        P("rep"),
        P("rep", None),
        P("rep"),
        P(None, "rep"),
        P(),
    )
    out_specs = (
        P(None, "blk", "gy", "rep"),
        P(),
        P("rep", None),
        P("rep"),
        P("rep", None),
        P("rep"),
        P(None, "rep"),
        P(),
        P(None, "blk", "gy", "rep"),
    )
    return jax.shard_map(
        per_device, mesh=mesh, in_specs=in_specs, out_specs=out_specs, check_vma=False
    )
```

profile of v0, /device:TPU:1, one launch (start us, length us, event | category | flops | bytes accessed | tf_op | source)
XLA Modules:
  0.0 383.7 jit_solution(16146299786309421557)
XLA Ops:
  5.6 13.3 %all_gather.3 = bf16[64,82]{1,0:T(8,128)(2,1)S(1)} all-gather(bf16[16,82]{1,0:T(8,128)(2,1)S(1)} %concatenate.347), channel_id=1, replica_groups=mesh['blk'=32,'gy'=4,'rep'=4] {'rep'}, dimensions={0}, use_global_device_ids=true | all-gather | bytes 13120 | tf_op jit(solution)/shard_map/all_gather | solution.py:122
  30.3 7.8 %collective-permute-start.4 = (f32[4,1,8,128]{3,2,1,0:T(8,128)S(1)}, f32[4,1,8,128]{3,2,1,0:T(8,128)S(1)}, u32[]{:S(2)}, u32[]{:S(2)}) collective-permute-start(f32[4,1,8,128]{3,2,1,0:T(8,128)S(1)} %get-tuple-element.85), channel_id=1, source_target_pairs={{16,0},{32,16},{48,32},{64,48},{80,64},{96,80},{112,96},{128,112},... | collective-permute-start | bytes 49160 | tf_op jit(solution)/shard_map/ppermute | solution.py:25
  43.1 4.2 %collective-permute-done = f32[4,4,8,1]{3,2,1,0:T(8,128)S(1)} collective-permute-done((f32[4,4,8,1]{3,2,1,0:T(8,128)S(1)}, f32[4,4,8,1]{3,2,1,0:T(8,128)S(1)}, u32[]{:S(2)}, u32[]{:S(2)}) %collective-permute-start) | collective-permute-done | bytes 544 | tf_op jit(solution)/shard_map/ppermute | solution.py:25
  54.9 5.5 %collective-permute-start.6 = (f32[4,4,8,1]{3,2,1,0:T(8,128)S(1)}, f32[4,4,8,1]{3,2,1,0:T(8,128)S(1)}, u32[]{:S(2)}, u32[]{:S(2)}) collective-permute-start(f32[4,4,8,1]{3,2,1,0:T(8,128)S(1)} %get-tuple-element.69), channel_id=1, source_target_pairs={{1,0},{2,1},{3,2},{0,3},{5,4},{6,5},{7,6},{4,7},{9,8},{10,9},{11,1... | collective-permute-start | bytes 1544 | tf_op jit(solution)/shard_map/ppermute | solution.py:25
  60.4 4.6 %collective-permute-start.8 = (f32[4,4,1,128]{3,2,1,0:T(1,128)S(1)}, f32[4,4,1,128]{3,2,1,0:T(1,128)S(1)}, u32[]{:S(2)}, u32[]{:S(2)}) collective-permute-start(f32[4,4,1,128]{3,2,1,0:T(1,128)S(1)} %get-tuple-element.73), channel_id=1, source_target_pairs={{4,0},{8,4},{12,8},{0,12},{5,1},{9,5},{13,9},{1,13},{6,2},{10,6},{... | collective-permute-start | bytes 24584 | tf_op jit(solution)/shard_map/ppermute | solution.py:25
  66.9 4.9 %collective-permute-start.10 = (f32[4,1,8,128]{3,2,1,0:T(8,128)S(1)}, f32[4,1,8,128]{3,2,1,0:T(8,128)S(1)}, u32[]{:S(2)}, u32[]{:S(2)}) collective-permute-start(f32[4,1,8,128]{3,2,1,0:T(8,128)S(1)} %get-tuple-element.75), channel_id=1, source_target_pairs={{16,0},{32,16},{48,32},{64,48},{80,64},{96,80},{112,96},{128,112},... | collective-permute-start | bytes 49160 | tf_op jit(solution)/shard_map/ppermute | solution.py:25
  73.7 3.9 %collective-permute-start.7 = (f32[4,4,8,1]{3,2,1,0:T(8,128)S(1)}, f32[4,4,8,1]{3,2,1,0:T(8,128)S(1)}, u32[]{:S(2)}, u32[]{:S(2)}) collective-permute-start(f32[4,4,8,1]{3,2,1,0:T(8,128)S(1)} %get-tuple-element.70), channel_id=1, source_target_pairs={{0,1},{1,2},{2,3},{3,0},{4,5},{5,6},{6,7},{7,4},{8,9},{9,10},{10,1... | collective-permute-start | bytes 1544 | tf_op jit(solution)/shard_map/ppermute | solution.py:24
  83.5 4.3 %collective-permute-start.12 = (f32[4,4,8,1]{3,2,1,0:T(8,128)S(1)}, f32[4,4,8,1]{3,2,1,0:T(8,128)S(1)}, u32[]{:S(2)}, u32[]{:S(2)}) collective-permute-start(f32[4,4,8,1]{3,2,1,0:T(8,128)S(1)} %get-tuple-element.59), channel_id=1, source_target_pairs={{1,0},{2,1},{3,2},{0,3},{5,4},{6,5},{7,6},{4,7},{9,8},{10,9},{11,1... | collective-permute-start | bytes 1544 | tf_op jit(solution)/shard_map/ppermute | solution.py:25
  87.8 4.8 %collective-permute-start.14 = (f32[4,4,1,128]{3,2,1,0:T(1,128)S(1)}, f32[4,4,1,128]{3,2,1,0:T(1,128)S(1)}, u32[]{:S(2)}, u32[]{:S(2)}) collective-permute-start(f32[4,4,1,128]{3,2,1,0:T(1,128)S(1)} %get-tuple-element.63), channel_id=1, source_target_pairs={{4,0},{8,4},{12,8},{0,12},{5,1},{9,5},{13,9},{1,13},{6,2},{10,6},{... | collective-permute-start | bytes 24584 | tf_op jit(solution)/shard_map/ppermute | solution.py:25
  94.6 5.8 %collective-permute-start.16 = (f32[4,1,8,128]{3,2,1,0:T(8,128)S(1)}, f32[4,1,8,128]{3,2,1,0:T(8,128)S(1)}, u32[]{:S(2)}, u32[]{:S(2)}) collective-permute-start(f32[4,1,8,128]{3,2,1,0:T(8,128)S(1)} %get-tuple-element.65), channel_id=1, source_target_pairs={{16,0},{32,16},{48,32},{64,48},{80,64},{96,80},{112,96},{128,112},... | collective-permute-start | bytes 49160 | tf_op jit(solution)/shard_map/ppermute | solution.py:25
  102.3 3.9 %collective-permute-start.13 = (f32[4,4,8,1]{3,2,1,0:T(8,128)S(1)}, f32[4,4,8,1]{3,2,1,0:T(8,128)S(1)}, u32[]{:S(2)}, u32[]{:S(2)}) collective-permute-start(f32[4,4,8,1]{3,2,1,0:T(8,128)S(1)} %get-tuple-element.60), channel_id=1, source_target_pairs={{0,1},{1,2},{2,3},{3,0},{4,5},{5,6},{6,7},{7,4},{8,9},{9,10},{10,1... | collective-permute-start | bytes 1544 | tf_op jit(solution)/shard_map/ppermute | solution.py:24
  111.7 4.3 %collective-permute-start.18 = (f32[4,4,8,1]{3,2,1,0:T(8,128)S(1)}, f32[4,4,8,1]{3,2,1,0:T(8,128)S(1)}, u32[]{:S(2)}, u32[]{:S(2)}) collective-permute-start(f32[4,4,8,1]{3,2,1,0:T(8,128)S(1)} %get-tuple-element.49), channel_id=1, source_target_pairs={{1,0},{2,1},{3,2},{0,3},{5,4},{6,5},{7,6},{4,7},{9,8},{10,9},{11,1... | collective-permute-start | bytes 1544 | tf_op jit(solution)/shard_map/ppermute | solution.py:25
  116.0 4.9 %collective-permute-start.20 = (f32[4,4,1,128]{3,2,1,0:T(1,128)S(1)}, f32[4,4,1,128]{3,2,1,0:T(1,128)S(1)}, u32[]{:S(2)}, u32[]{:S(2)}) collective-permute-start(f32[4,4,1,128]{3,2,1,0:T(1,128)S(1)} %get-tuple-element.53), channel_id=1, source_target_pairs={{4,0},{8,4},{12,8},{0,12},{5,1},{9,5},{13,9},{1,13},{6,2},{10,6},{... | collective-permute-start | bytes 24584 | tf_op jit(solution)/shard_map/ppermute | solution.py:25
  122.8 5.8 %collective-permute-start.22 = (f32[4,1,8,128]{3,2,1,0:T(8,128)S(1)}, f32[4,1,8,128]{3,2,1,0:T(8,128)S(1)}, u32[]{:S(2)}, u32[]{:S(2)}) collective-permute-start(f32[4,1,8,128]{3,2,1,0:T(8,128)S(1)} %get-tuple-element.55), channel_id=1, source_target_pairs={{16,0},{32,16},{48,32},{64,48},{80,64},{96,80},{112,96},{128,112},... | collective-permute-start | bytes 49160 | tf_op jit(solution)/shard_map/ppermute | solution.py:25
  140.1 4.8 %collective-permute-start.26 = (f32[2,4,1,128]{3,2,1,0:T(1,128)}, f32[2,4,1,128]{3,2,1,0:T(1,128)}, u32[]{:S(2)}, u32[]{:S(2)}) collective-permute-start(f32[2,4,1,128]{3,2,1,0:T(1,128)} %get-tuple-element.129), channel_id=1, source_target_pairs={{4,0},{8,4},{12,8},{0,12},{5,1},{9,5},{13,9},{1,13},{6,2},{10,6},{... | collective-permute-start | bytes 12296 | tf_op jit(solution)/shard_map/ppermute | solution.py:25
  147.5 5.1 %collective-permute-start.28 = (f32[2,1,8,128]{3,2,1,0:T(8,128)}, f32[2,1,8,128]{3,2,1,0:T(8,128)}, u32[]{:S(2)}, u32[]{:S(2)}) collective-permute-start(f32[2,1,8,128]{3,2,1,0:T(8,128)} %get-tuple-element.133), channel_id=1, source_target_pairs={{16,0},{32,16},{48,32},{64,48},{80,64},{96,80},{112,96},{128,112},... | collective-permute-start | bytes 24584 | tf_op jit(solution)/shard_map/ppermute | solution.py:25
  152.6 5.5 %collective-permute-start.24 = (f32[2,4,8,1]{3,2,1,0:T(8,128)}, f32[2,4,8,1]{3,2,1,0:T(8,128)}, u32[]{:S(2)}, u32[]{:S(2)}) collective-permute-start(f32[2,4,8,1]{3,2,1,0:T(8,128)} %get-tuple-element.125), channel_id=1, source_target_pairs={{1,0},{2,1},{3,2},{0,3},{5,4},{6,5},{7,6},{4,7},{9,8},{10,9},{11,1... | collective-permute-start | bytes 776 | tf_op jit(solution)/shard_map/ppermute | solution.py:25
  181.7 4.8 %collective-permute-start.32 = (f32[2,4,1,128]{3,2,1,0:T(1,128)S(1)}, f32[2,4,1,128]{3,2,1,0:T(1,128)S(1)}, u32[]{:S(2)}, u32[]{:S(2)}) collective-permute-start(f32[2,4,1,128]{3,2,1,0:T(1,128)S(1)} %get-tuple-element.117), channel_id=1, source_target_pairs={{4,0},{8,4},{12,8},{0,12},{5,1},{9,5},{13,9},{1,13},{6,2},{10,6},{... | collective-permute-start | bytes 12296 | tf_op jit(solution)/shard_map/ppermute | solution.py:25
  190.9 4.7 %collective-permute-start.31 = (f32[2,4,8,1]{3,2,1,0:T(8,128)S(1)}, f32[2,4,8,1]{3,2,1,0:T(8,128)S(1)}, u32[]{:S(2)}, u32[]{:S(2)}) collective-permute-start(f32[2,4,8,1]{3,2,1,0:T(8,128)S(1)} %get-tuple-element.114), channel_id=1, source_target_pairs={{0,1},{1,2},{2,3},{3,0},{4,5},{5,6},{6,7},{7,4},{8,9},{9,10},{10,1... | collective-permute-start | bytes 776 | tf_op jit(solution)/shard_map/ppermute | solution.py:24
  216.0 4.6 %collective-permute-start.38 = (f32[2,4,1,128]{3,2,1,0:T(1,128)S(1)}, f32[2,4,1,128]{3,2,1,0:T(1,128)S(1)}, u32[]{:S(2)}, u32[]{:S(2)}) collective-permute-start(f32[2,4,1,128]{3,2,1,0:T(1,128)S(1)} %get-tuple-element.105), channel_id=1, source_target_pairs={{4,0},{8,4},{12,8},{0,12},{5,1},{9,5},{13,9},{1,13},{6,2},{10,6},{... | collective-permute-start | bytes 12296 | tf_op jit(solution)/shard_map/ppermute | solution.py:25
  224.4 5.1 %collective-permute-start.37 = (f32[2,4,8,1]{3,2,1,0:T(8,128)S(1)}, f32[2,4,8,1]{3,2,1,0:T(8,128)S(1)}, u32[]{:S(2)}, u32[]{:S(2)}) collective-permute-start(f32[2,4,8,1]{3,2,1,0:T(8,128)S(1)} %get-tuple-element.102), channel_id=1, source_target_pairs={{0,1},{1,2},{2,3},{3,0},{4,5},{5,6},{6,7},{7,4},{8,9},{9,10},{10,1... | collective-permute-start | bytes 776 | tf_op jit(solution)/shard_map/ppermute | solution.py:24
  249.8 4.6 %collective-permute-start.44 = (f32[2,4,1,128]{3,2,1,0:T(1,128)S(1)}, f32[2,4,1,128]{3,2,1,0:T(1,128)S(1)}, u32[]{:S(2)}, u32[]{:S(2)}) collective-permute-start(f32[2,4,1,128]{3,2,1,0:T(1,128)S(1)} %get-tuple-element.93), channel_id=1, source_target_pairs={{4,0},{8,4},{12,8},{0,12},{5,1},{9,5},{13,9},{1,13},{6,2},{10,6},{... | collective-permute-start | bytes 12296 | tf_op jit(solution)/shard_map/ppermute | solution.py:25
  258.5 4.8 %collective-permute-start.43 = (f32[2,4,8,1]{3,2,1,0:T(8,128)S(1)}, f32[2,4,8,1]{3,2,1,0:T(8,128)S(1)}, u32[]{:S(2)}, u32[]{:S(2)}) collective-permute-start(f32[2,4,8,1]{3,2,1,0:T(8,128)S(1)} %get-tuple-element.90), channel_id=1, source_target_pairs={{0,1},{1,2},{2,3},{3,0},{4,5},{5,6},{6,7},{7,4},{8,9},{9,10},{10,1... | collective-permute-start | bytes 776 | tf_op jit(solution)/shard_map/ppermute | solution.py:24
  276.9 101.3 %psum.7 = f32[5255]{0:T(1024)S(1)} all-reduce(f32[5255]{0:T(1024)S(1)} %concatenate.436), channel_id=1, replica_groups=mesh['blk'=32,'gy'=4,'rep'=4] {'blk','gy','rep'}, use_global_device_ids=true, to_apply=%region_13.0 | all-reduce | flops 5255 | bytes 42040 | tf_op jit(solution)/shard_map/psum | solution.py:188
  (875 shorter events, 153.9 us)
Async XLA Ops:
  25.0 25.5 %collective-permute-start.2 = (f32[4,4,1,128]{3,2,1,0:T(1,128)S(1)}, f32[4,4,1,128]{3,2,1,0:T(1,128)S(1)}, u32[]{:S(2)}, u32[]{:S(2)}) collective-permute-start(f32[4,4,1,128]{3,2,1,0:T(1,128)S(1)} %get-tuple-element.83), channel_id=1, source_target_pairs={{4,0},{8,4},{12,8},{0,12},{5,1},{9,5},{13,9},{1,13},{6,2},{10,6},{... | collective-permute-start | bytes 24584 | tf_op jit(solution)/shard_map/ppermute | solution.py:25
  26.9 23.6 %collective-permute-start.3 = (f32[4,4,1,128]{3,2,1,0:T(1,128)S(1)}, f32[4,4,1,128]{3,2,1,0:T(1,128)S(1)}, u32[]{:S(2)}, u32[]{:S(2)}) collective-permute-start(f32[4,4,1,128]{3,2,1,0:T(1,128)S(1)} %get-tuple-element.84), channel_id=1, source_target_pairs={{0,4},{4,8},{8,12},{12,0},{1,5},{5,9},{9,13},{13,1},{2,6},{6,10},{... | collective-permute-start | bytes 24584 | tf_op jit(solution)/shard_map/ppermute | solution.py:24
  30.3 20.2 %collective-permute-start.4 = (f32[4,1,8,128]{3,2,1,0:T(8,128)S(1)}, f32[4,1,8,128]{3,2,1,0:T(8,128)S(1)}, u32[]{:S(2)}, u32[]{:S(2)}) collective-permute-start(f32[4,1,8,128]{3,2,1,0:T(8,128)S(1)} %get-tuple-element.85), channel_id=1, source_target_pairs={{16,0},{32,16},{48,32},{64,48},{80,64},{96,80},{112,96},{128,112},... | collective-permute-start | bytes 49160 | tf_op jit(solution)/shard_map/ppermute | solution.py:25
  38.1 12.5 %collective-permute-start.5 = (f32[4,1,8,128]{3,2,1,0:T(8,128)S(1)}, f32[4,1,8,128]{3,2,1,0:T(8,128)S(1)}, u32[]{:S(2)}, u32[]{:S(2)}) collective-permute-start(f32[4,1,8,128]{3,2,1,0:T(8,128)S(1)} %get-tuple-element.86), channel_id=1, source_target_pairs={{0,16},{16,32},{32,48},{48,64},{64,80},{80,96},{96,112},{112,128},... | collective-permute-start | bytes 49160 | tf_op jit(solution)/shard_map/ppermute | solution.py:24
  54.9 18.8 %collective-permute-start.6 = (f32[4,4,8,1]{3,2,1,0:T(8,128)S(1)}, f32[4,4,8,1]{3,2,1,0:T(8,128)S(1)}, u32[]{:S(2)}, u32[]{:S(2)}) collective-permute-start(f32[4,4,8,1]{3,2,1,0:T(8,128)S(1)} %get-tuple-element.69), channel_id=1, source_target_pairs={{1,0},{2,1},{3,2},{0,3},{5,4},{6,5},{7,6},{4,7},{9,8},{10,9},{11,1... | collective-permute-start | bytes 1544 | tf_op jit(solution)/shard_map/ppermute | solution.py:25
  60.4 18.6 %collective-permute-start.8 = (f32[4,4,1,128]{3,2,1,0:T(1,128)S(1)}, f32[4,4,1,128]{3,2,1,0:T(1,128)S(1)}, u32[]{:S(2)}, u32[]{:S(2)}) collective-permute-start(f32[4,4,1,128]{3,2,1,0:T(1,128)S(1)} %get-tuple-element.73), channel_id=1, source_target_pairs={{4,0},{8,4},{12,8},{0,12},{5,1},{9,5},{13,9},{1,13},{6,2},{10,6},{... | collective-permute-start | bytes 24584 | tf_op jit(solution)/shard_map/ppermute | solution.py:25
  65.0 14.1 %collective-permute-start.9 = (f32[4,4,1,128]{3,2,1,0:T(1,128)S(1)}, f32[4,4,1,128]{3,2,1,0:T(1,128)S(1)}, u32[]{:S(2)}, u32[]{:S(2)}) collective-permute-start(f32[4,4,1,128]{3,2,1,0:T(1,128)S(1)} %get-tuple-element.74), channel_id=1, source_target_pairs={{0,4},{4,8},{8,12},{12,0},{1,5},{5,9},{9,13},{13,1},{2,6},{6,10},{... | collective-permute-start | bytes 24584 | tf_op jit(solution)/shard_map/ppermute | solution.py:24
  83.5 18.8 %collective-permute-start.12 = (f32[4,4,8,1]{3,2,1,0:T(8,128)S(1)}, f32[4,4,8,1]{3,2,1,0:T(8,128)S(1)}, u32[]{:S(2)}, u32[]{:S(2)}) collective-permute-start(f32[4,4,8,1]{3,2,1,0:T(8,128)S(1)} %get-tuple-element.59), channel_id=1, source_target_pairs={{1,0},{2,1},{3,2},{0,3},{5,4},{6,5},{7,6},{4,7},{9,8},{10,9},{11,1... | collective-permute-start | bytes 1544 | tf_op jit(solution)/shard_map/ppermute | solution.py:25
  87.8 19.8 %collective-permute-start.14 = (f32[4,4,1,128]{3,2,1,0:T(1,128)S(1)}, f32[4,4,1,128]{3,2,1,0:T(1,128)S(1)}, u32[]{:S(2)}, u32[]{:S(2)}) collective-permute-start(f32[4,4,1,128]{3,2,1,0:T(1,128)S(1)} %get-tuple-element.63), channel_id=1, source_target_pairs={{4,0},{8,4},{12,8},{0,12},{5,1},{9,5},{13,9},{1,13},{6,2},{10,6},{... | collective-permute-start | bytes 24584 | tf_op jit(solution)/shard_map/ppermute | solution.py:25
  92.6 15.0 %collective-permute-start.15 = (f32[4,4,1,128]{3,2,1,0:T(1,128)S(1)}, f32[4,4,1,128]{3,2,1,0:T(1,128)S(1)}, u32[]{:S(2)}, u32[]{:S(2)}) collective-permute-start(f32[4,4,1,128]{3,2,1,0:T(1,128)S(1)} %get-tuple-element.64), channel_id=1, source_target_pairs={{0,4},{4,8},{8,12},{12,0},{1,5},{5,9},{9,13},{13,1},{2,6},{6,10},{... | collective-permute-start | bytes 24584 | tf_op jit(solution)/shard_map/ppermute | solution.py:24
  94.6 13.1 %collective-permute-start.16 = (f32[4,1,8,128]{3,2,1,0:T(8,128)S(1)}, f32[4,1,8,128]{3,2,1,0:T(8,128)S(1)}, u32[]{:S(2)}, u32[]{:S(2)}) collective-permute-start(f32[4,1,8,128]{3,2,1,0:T(8,128)S(1)} %get-tuple-element.65), channel_id=1, source_target_pairs={{16,0},{32,16},{48,32},{64,48},{80,64},{96,80},{112,96},{128,112},... | collective-permute-start | bytes 49160 | tf_op jit(solution)/shard_map/ppermute | solution.py:25
  111.7 18.8 %collective-permute-start.18 = (f32[4,4,8,1]{3,2,1,0:T(8,128)S(1)}, f32[4,4,8,1]{3,2,1,0:T(8,128)S(1)}, u32[]{:S(2)}, u32[]{:S(2)}) collective-permute-start(f32[4,4,8,1]{3,2,1,0:T(8,128)S(1)} %get-tuple-element.49), channel_id=1, source_target_pairs={{1,0},{2,1},{3,2},{0,3},{5,4},{6,5},{7,6},{4,7},{9,8},{10,9},{11,1... | collective-permute-start | bytes 1544 | tf_op jit(solution)/shard_map/ppermute | solution.py:25
  116.0 19.8 %collective-permute-start.20 = (f32[4,4,1,128]{3,2,1,0:T(1,128)S(1)}, f32[4,4,1,128]{3,2,1,0:T(1,128)S(1)}, u32[]{:S(2)}, u32[]{:S(2)}) collective-permute-start(f32[4,4,1,128]{3,2,1,0:T(1,128)S(1)} %get-tuple-element.53), channel_id=1, source_target_pairs={{4,0},{8,4},{12,8},{0,12},{5,1},{9,5},{13,9},{1,13},{6,2},{10,6},{... | collective-permute-start | bytes 24584 | tf_op jit(solution)/shard_map/ppermute | solution.py:25
  120.9 15.0 %collective-permute-start.21 = (f32[4,4,1,128]{3,2,1,0:T(1,128)S(1)}, f32[4,4,1,128]{3,2,1,0:T(1,128)S(1)}, u32[]{:S(2)}, u32[]{:S(2)}) collective-permute-start(f32[4,4,1,128]{3,2,1,0:T(1,128)S(1)} %get-tuple-element.54), channel_id=1, source_target_pairs={{0,4},{4,8},{8,12},{12,0},{1,5},{5,9},{9,13},{13,1},{2,6},{6,10},{... | collective-permute-start | bytes 24584 | tf_op jit(solution)/shard_map/ppermute | solution.py:24
  122.8 13.1 %collective-permute-start.22 = (f32[4,1,8,128]{3,2,1,0:T(8,128)S(1)}, f32[4,1,8,128]{3,2,1,0:T(8,128)S(1)}, u32[]{:S(2)}, u32[]{:S(2)}) collective-permute-start(f32[4,1,8,128]{3,2,1,0:T(8,128)S(1)} %get-tuple-element.55), channel_id=1, source_target_pairs={{16,0},{32,16},{48,32},{64,48},{80,64},{96,80},{112,96},{128,112},... | collective-permute-start | bytes 49160 | tf_op jit(solution)/shard_map/ppermute | solution.py:25
  140.1 24.1 %collective-permute-start.26 = (f32[2,4,1,128]{3,2,1,0:T(1,128)}, f32[2,4,1,128]{3,2,1,0:T(1,128)}, u32[]{:S(2)}, u32[]{:S(2)}) collective-permute-start(f32[2,4,1,128]{3,2,1,0:T(1,128)} %get-tuple-element.129), channel_id=1, source_target_pairs={{4,0},{8,4},{12,8},{0,12},{5,1},{9,5},{13,9},{1,13},{6,2},{10,6},{... | collective-permute-start | bytes 12296 | tf_op jit(solution)/shard_map/ppermute | solution.py:25
  144.9 19.2 %collective-permute-start.27 = (f32[2,4,1,128]{3,2,1,0:T(1,128)}, f32[2,4,1,128]{3,2,1,0:T(1,128)}, u32[]{:S(2)}, u32[]{:S(2)}) collective-permute-start(f32[2,4,1,128]{3,2,1,0:T(1,128)} %get-tuple-element.130), channel_id=1, source_target_pairs={{0,4},{4,8},{8,12},{12,0},{1,5},{5,9},{9,13},{13,1},{2,6},{6,10},{... | collective-permute-start | bytes 12296 | tf_op jit(solution)/shard_map/ppermute | solution.py:24
  147.5 17.7 %collective-permute-start.28 = (f32[2,1,8,128]{3,2,1,0:T(8,128)}, f32[2,1,8,128]{3,2,1,0:T(8,128)}, u32[]{:S(2)}, u32[]{:S(2)}) collective-permute-start(f32[2,1,8,128]{3,2,1,0:T(8,128)} %get-tuple-element.133), channel_id=1, source_target_pairs={{16,0},{32,16},{48,32},{64,48},{80,64},{96,80},{112,96},{128,112},... | collective-permute-start | bytes 24584 | tf_op jit(solution)/shard_map/ppermute | solution.py:25
  181.7 19.4 %collective-permute-start.32 = (f32[2,4,1,128]{3,2,1,0:T(1,128)S(1)}, f32[2,4,1,128]{3,2,1,0:T(1,128)S(1)}, u32[]{:S(2)}, u32[]{:S(2)}) collective-permute-start(f32[2,4,1,128]{3,2,1,0:T(1,128)S(1)} %get-tuple-element.117), channel_id=1, source_target_pairs={{4,0},{8,4},{12,8},{0,12},{5,1},{9,5},{13,9},{1,13},{6,2},{10,6},{... | collective-permute-start | bytes 12296 | tf_op jit(solution)/shard_map/ppermute | solution.py:25
  186.6 14.6 %collective-permute-start.33 = (f32[2,4,1,128]{3,2,1,0:T(1,128)S(1)}, f32[2,4,1,128]{3,2,1,0:T(1,128)S(1)}, u32[]{:S(2)}, u32[]{:S(2)}) collective-permute-start(f32[2,4,1,128]{3,2,1,0:T(1,128)S(1)} %get-tuple-element.118), channel_id=1, source_target_pairs={{0,4},{4,8},{8,12},{12,0},{1,5},{5,9},{9,13},{13,1},{2,6},{6,10},{... | collective-permute-start | bytes 12296 | tf_op jit(solution)/shard_map/ppermute | solution.py:24
  216.0 18.9 %collective-permute-start.38 = (f32[2,4,1,128]{3,2,1,0:T(1,128)S(1)}, f32[2,4,1,128]{3,2,1,0:T(1,128)S(1)}, u32[]{:S(2)}, u32[]{:S(2)}) collective-permute-start(f32[2,4,1,128]{3,2,1,0:T(1,128)S(1)} %get-tuple-element.105), channel_id=1, source_target_pairs={{4,0},{8,4},{12,8},{0,12},{5,1},{9,5},{13,9},{1,13},{6,2},{10,6},{... | collective-permute-start | bytes 12296 | tf_op jit(solution)/shard_map/ppermute | solution.py:25
  220.5 14.4 %collective-permute-start.39 = (f32[2,4,1,128]{3,2,1,0:T(1,128)S(1)}, f32[2,4,1,128]{3,2,1,0:T(1,128)S(1)}, u32[]{:S(2)}, u32[]{:S(2)}) collective-permute-start(f32[2,4,1,128]{3,2,1,0:T(1,128)S(1)} %get-tuple-element.106), channel_id=1, source_target_pairs={{0,4},{4,8},{8,12},{12,0},{1,5},{5,9},{9,13},{13,1},{2,6},{6,10},{... | collective-permute-start | bytes 12296 | tf_op jit(solution)/shard_map/ppermute | solution.py:24
  249.8 18.9 %collective-permute-start.44 = (f32[2,4,1,128]{3,2,1,0:T(1,128)S(1)}, f32[2,4,1,128]{3,2,1,0:T(1,128)S(1)}, u32[]{:S(2)}, u32[]{:S(2)}) collective-permute-start(f32[2,4,1,128]{3,2,1,0:T(1,128)S(1)} %get-tuple-element.93), channel_id=1, source_target_pairs={{4,0},{8,4},{12,8},{0,12},{5,1},{9,5},{13,9},{1,13},{6,2},{10,6},{... | collective-permute-start | bytes 12296 | tf_op jit(solution)/shard_map/ppermute | solution.py:25
  254.3 14.4 %collective-permute-start.45 = (f32[2,4,1,128]{3,2,1,0:T(1,128)S(1)}, f32[2,4,1,128]{3,2,1,0:T(1,128)S(1)}, u32[]{:S(2)}, u32[]{:S(2)}) collective-permute-start(f32[2,4,1,128]{3,2,1,0:T(1,128)S(1)} %get-tuple-element.94), channel_id=1, source_target_pairs={{0,4},{4,8},{8,12},{12,0},{1,5},{5,9},{9,13},{13,1},{2,6},{6,10},{... | collective-permute-start | bytes 12296 | tf_op jit(solution)/shard_map/ppermute | solution.py:24
  (324 other events, 5158.2 us)
where the time goes:
time: 386 us; the launch traced here: 384 us
  starting transfers between devices  167 us (43%)
  blocking collectives  115 us (30%)
  matrix products  34.2 us (9%)
  local copies, waits for them, and re-layouts  22.1 us (6%)
  waiting for transfers between devices  21.5 us (6%)
  other arithmetic  17.5 us (5%)
  between operations  6.61 us (2%)
    psum x1, blocking collectives, per_device(): summed_flat = lax.psum(flat, ('blk', 'gy', 'rep'))  101 us
    ppermute x24, starting transfers between devices, exchange_faces(): high = lax.ppermute(lax.slice_in_dim(block, 0, 1, axis=dim), axis, backward)  98.7 us
    ppermute x24, starting transfers between devices, exchange_faces(): lax.ppermute(lax.slice_in_dim(block, size - 1, size, axis=dim), axis, for...  68.5 us
    ppermute x24, waiting for transfers between devices, exchange_faces(): lax.ppermute(lax.slice_in_dim(block, size - 1, size, axis=dim), axis, for...  17.3 us
    all_gather x1, blocking collectives, gather_params(): full = lax.all_gather(packed, 'rep', axis=0, tiled=True)  13.3 us
  transfers between devices with their start and end apart: 48, of which 9 were waited for; matrix products, arithmetic and copies ran while one was open for 1% of the time, Pallas kernels for 0%

commit v1 on v0

--- a/solution.py
+++ b/solution.py
@@ -185,7 +185,7 @@
     start_sensitivity = adjoint * (2.0 * total_cells)
     pieces = list(grad_sums) + [loss_part[None]]
     flat = jnp.concatenate([piece.reshape(-1) for piece in pieces])
-    summed_flat = lax.psum(flat, ("blk", "gy", "rep"))
+    summed_flat = lax.psum(lax.psum(flat, "blk"), ("gy", "rep"))
     summed = []
     start = 0
     for piece in pieces:

time: 386 us -> 467 us (1.21); the launches traced: 384 us -> 460 us
  blocking collectives: 115 us -> 191 us
    psum x1 -> x2, blocking collectives: 101 us -> 177 us  [per_device(): summed_flat = lax.psum(lax.psum(flat, 'blk'), ('gy', 'rep'))]
where the time goes in v1:
time: 467 us; the launch traced here: 460 us
  blocking collectives  191 us (41%)
  starting transfers between devices  167 us (36%)
  matrix products  34.2 us (7%)
  local copies, waits for them, and re-layouts  22 us (5%)
  waiting for transfers between devices  21.5 us (5%)
  other arithmetic  17.5 us (4%)
  between operations  6.61 us (1%)
    psum x2, blocking collectives, per_device(): summed_flat = lax.psum(lax.psum(flat, 'blk'), ('gy', 'rep'))  177 us
    ppermute x24, starting transfers between devices, exchange_faces(): high = lax.ppermute(lax.slice_in_dim(block, 0, 1, axis=dim), axis, backward)  98.6 us
    ppermute x24, starting transfers between devices, exchange_faces(): lax.ppermute(lax.slice_in_dim(block, size - 1, size, axis=dim), axis, for...  68.6 us
    ppermute x24, waiting for transfers between devices, exchange_faces(): lax.ppermute(lax.slice_in_dim(block, size - 1, size, axis=dim), axis, for...  17.3 us
    all_gather x1, blocking collectives, gather_params(): full = lax.all_gather(packed, 'rep', axis=0, tiled=True)  13.3 us
  transfers between devices with their start and end apart: 48, of which 9 were waited for; matrix products, arithmetic and copies ran while one was open for 1% of the time, Pallas kernels for 0%

profile of v1, /device:TPU:1, one launch (start us, length us, event | category | flops | bytes accessed | tf_op | source)
XLA Modules:
  0.0 459.8 jit_solution(5671168981674032787)
XLA Ops:
  5.6 13.3 %all_gather.3 = bf16[64,82]{1,0:T(8,128)(2,1)S(1)} all-gather(bf16[16,82]{1,0:T(8,128)(2,1)S(1)} %concatenate.347), channel_id=1, replica_groups=mesh['blk'=32,'gy'=4,'rep'=4] {'rep'}, dimensions={0}, use_global_device_ids=true | all-gather | bytes 13120 | tf_op jit(solution)/shard_map/all_gather | solution.py:122
  30.3 7.8 %collective-permute-start.4 = (f32[4,1,8,128]{3,2,1,0:T(8,128)S(1)}, f32[4,1,8,128]{3,2,1,0:T(8,128)S(1)}, u32[]{:S(2)}, u32[]{:S(2)}) collective-permute-start(f32[4,1,8,128]{3,2,1,0:T(8,128)S(1)} %get-tuple-element.85), channel_id=1, source_target_pairs={{16,0},{32,16},{48,32},{64,48},{80,64},{96,80},{112,96},{128,112},... | collective-permute-start | bytes 49160 | tf_op jit(solution)/shard_map/ppermute | solution.py:25
  43.1 4.2 collective-permute-done
  54.9 5.5 %collective-permute-start.6 = (f32[4,4,8,1]{3,2,1,0:T(8,128)S(1)}, f32[4,4,8,1]{3,2,1,0:T(8,128)S(1)}, u32[]{:S(2)}, u32[]{:S(2)}) collective-permute-start(f32[4,4,8,1]{3,2,1,0:T(8,128)S(1)} %get-tuple-element.69), channel_id=1, source_target_pairs={{1,0},{2,1},{3,2},{0,3},{5,4},{6,5},{7,6},{4,7},{9,8},{10,9},{11,1... | collective-permute-start | bytes 1544 | tf_op jit(solution)/shard_map/ppermute | solution.py:25
  60.4 4.6 collective-permute-start.8
  66.9 4.9 %collective-permute-start.10 = (f32[4,1,8,128]{3,2,1,0:T(8,128)S(1)}, f32[4,1,8,128]{3,2,1,0:T(8,128)S(1)}, u32[]{:S(2)}, u32[]{:S(2)}) collective-permute-start(f32[4,1,8,128]{3,2,1,0:T(8,128)S(1)} %get-tuple-element.75), channel_id=1, source_target_pairs={{16,0},{32,16},{48,32},{64,48},{80,64},{96,80},{112,96},{128,112},... | collective-permute-start | bytes 49160 | tf_op jit(solution)/shard_map/ppermute | solution.py:25
  83.5 4.2 collective-permute-start.12
  87.8 4.9 %collective-permute-start.14 = (f32[4,4,1,128]{3,2,1,0:T(1,128)S(1)}, f32[4,4,1,128]{3,2,1,0:T(1,128)S(1)}, u32[]{:S(2)}, u32[]{:S(2)}) collective-permute-start(f32[4,4,1,128]{3,2,1,0:T(1,128)S(1)} %get-tuple-element.63), channel_id=1, source_target_pairs={{4,0},{8,4},{12,8},{0,12},{5,1},{9,5},{13,9},{1,13},{6,2},{10,6},{... | collective-permute-start | bytes 24584 | tf_op jit(solution)/shard_map/ppermute | solution.py:25
  94.6 5.8 %collective-permute-start.16 = (f32[4,1,8,128]{3,2,1,0:T(8,128)S(1)}, f32[4,1,8,128]{3,2,1,0:T(8,128)S(1)}, u32[]{:S(2)}, u32[]{:S(2)}) collective-permute-start(f32[4,1,8,128]{3,2,1,0:T(8,128)S(1)} %get-tuple-element.65), channel_id=1, source_target_pairs={{16,0},{32,16},{48,32},{64,48},{80,64},{96,80},{112,96},{128,112},... | collective-permute-start | bytes 49160 | tf_op jit(solution)/shard_map/ppermute | solution.py:25
  111.7 4.2 collective-permute-start.18
  116.0 4.9 %collective-permute-start.20 = (f32[4,4,1,128]{3,2,1,0:T(1,128)S(1)}, f32[4,4,1,128]{3,2,1,0:T(1,128)S(1)}, u32[]{:S(2)}, u32[]{:S(2)}) collective-permute-start(f32[4,4,1,128]{3,2,1,0:T(1,128)S(1)} %get-tuple-element.53), channel_id=1, source_target_pairs={{4,0},{8,4},{12,8},{0,12},{5,1},{9,5},{13,9},{1,13},{6,2},{10,6},{... | collective-permute-start | bytes 24584 | tf_op jit(solution)/shard_map/ppermute | solution.py:25
  122.8 5.7 %collective-permute-start.22 = (f32[4,1,8,128]{3,2,1,0:T(8,128)S(1)}, f32[4,1,8,128]{3,2,1,0:T(8,128)S(1)}, u32[]{:S(2)}, u32[]{:S(2)}) collective-permute-start(f32[4,1,8,128]{3,2,1,0:T(8,128)S(1)} %get-tuple-element.55), channel_id=1, source_target_pairs={{16,0},{32,16},{48,32},{64,48},{80,64},{96,80},{112,96},{128,112},... | collective-permute-start | bytes 49160 | tf_op jit(solution)/shard_map/ppermute | solution.py:25
  130.5 4.0 collective-permute-start.19
  140.1 4.8 %collective-permute-start.26 = (f32[2,4,1,128]{3,2,1,0:T(1,128)}, f32[2,4,1,128]{3,2,1,0:T(1,128)}, u32[]{:S(2)}, u32[]{:S(2)}) collective-permute-start(f32[2,4,1,128]{3,2,1,0:T(1,128)} %get-tuple-element.129), channel_id=1, source_target_pairs={{4,0},{8,4},{12,8},{0,12},{5,1},{9,5},{13,9},{1,13},{6,2},{10,6},{... | collective-permute-start | bytes 12296 | tf_op jit(solution)/shard_map/ppermute | solution.py:25
  147.5 5.1 %collective-permute-start.28 = (f32[2,1,8,128]{3,2,1,0:T(8,128)}, f32[2,1,8,128]{3,2,1,0:T(8,128)}, u32[]{:S(2)}, u32[]{:S(2)}) collective-permute-start(f32[2,1,8,128]{3,2,1,0:T(8,128)} %get-tuple-element.133), channel_id=1, source_target_pairs={{16,0},{32,16},{48,32},{64,48},{80,64},{96,80},{112,96},{128,112},... | collective-permute-start | bytes 24584 | tf_op jit(solution)/shard_map/ppermute | solution.py:25
  152.6 5.4 %collective-permute-start.24 = (f32[2,4,8,1]{3,2,1,0:T(8,128)}, f32[2,4,8,1]{3,2,1,0:T(8,128)}, u32[]{:S(2)}, u32[]{:S(2)}) collective-permute-start(f32[2,4,8,1]{3,2,1,0:T(8,128)} %get-tuple-element.125), channel_id=1, source_target_pairs={{1,0},{2,1},{3,2},{0,3},{5,4},{6,5},{7,6},{4,7},{9,8},{10,9},{11,1... | collective-permute-start | bytes 776 | tf_op jit(solution)/shard_map/ppermute | solution.py:25
  181.7 4.8 %collective-permute-start.32 = (f32[2,4,1,128]{3,2,1,0:T(1,128)S(1)}, f32[2,4,1,128]{3,2,1,0:T(1,128)S(1)}, u32[]{:S(2)}, u32[]{:S(2)}) collective-permute-start(f32[2,4,1,128]{3,2,1,0:T(1,128)S(1)} %get-tuple-element.117), channel_id=1, source_target_pairs={{4,0},{8,4},{12,8},{0,12},{5,1},{9,5},{13,9},{1,13},{6,2},{10,6},{... | collective-permute-start | bytes 12296 | tf_op jit(solution)/shard_map/ppermute | solution.py:25
  190.9 4.7 %collective-permute-start.31 = (f32[2,4,8,1]{3,2,1,0:T(8,128)S(1)}, f32[2,4,8,1]{3,2,1,0:T(8,128)S(1)}, u32[]{:S(2)}, u32[]{:S(2)}) collective-permute-start(f32[2,4,8,1]{3,2,1,0:T(8,128)S(1)} %get-tuple-element.114), channel_id=1, source_target_pairs={{0,1},{1,2},{2,3},{3,0},{4,5},{5,6},{6,7},{7,4},{8,9},{9,10},{10,1... | collective-permute-start | bytes 776 | tf_op jit(solution)/shard_map/ppermute | solution.py:24
  215.9 4.6 collective-permute-start.38
  224.4 5.1 %collective-permute-start.37 = (f32[2,4,8,1]{3,2,1,0:T(8,128)S(1)}, f32[2,4,8,1]{3,2,1,0:T(8,128)S(1)}, u32[]{:S(2)}, u32[]{:S(2)}) collective-permute-start(f32[2,4,8,1]{3,2,1,0:T(8,128)S(1)} %get-tuple-element.102), channel_id=1, source_target_pairs={{0,1},{1,2},{2,3},{3,0},{4,5},{5,6},{6,7},{7,4},{8,9},{9,10},{10,1... | collective-permute-start | bytes 776 | tf_op jit(solution)/shard_map/ppermute | solution.py:24
  249.8 4.6 collective-permute-start.44
  258.6 4.8 %collective-permute-start.43 = (f32[2,4,8,1]{3,2,1,0:T(8,128)S(1)}, f32[2,4,8,1]{3,2,1,0:T(8,128)S(1)}, u32[]{:S(2)}, u32[]{:S(2)}) collective-permute-start(f32[2,4,8,1]{3,2,1,0:T(8,128)S(1)} %get-tuple-element.90), channel_id=1, source_target_pairs={{0,1},{1,2},{2,3},{3,0},{4,5},{5,6},{6,7},{7,4},{8,9},{9,10},{10,1... | collective-permute-start | bytes 776 | tf_op jit(solution)/shard_map/ppermute | solution.py:24
  276.9 90.9 %psum.14 = f32[5255]{0:T(1024)S(1)} all-reduce(f32[5255]{0:T(1024)S(1)} %concatenate.436), channel_id=1, replica_groups=mesh['blk'=32,'gy'=4,'rep'=4] {'blk'}, use_global_device_ids=true, to_apply=%region_13.0 | all-reduce | flops 5255 | bytes 42040 | tf_op jit(solution)/shard_map/psum | solution.py:188
  367.9 86.4 %psum.15 = f32[5255]{0:T(1024)S(1)} all-reduce(f32[5255]{0:T(1024)S(1)} %psum.14), channel_id=1, replica_groups=mesh['blk'=32,'gy'=4,'rep'=4] {'gy','rep'}, use_global_device_ids=true, to_apply=%region_14.0 | all-reduce | flops 5255 | bytes 42040 | tf_op jit(solution)/shard_map/psum | solution.py:188
  (876 shorter events, 157.9 us)
Async XLA Ops:
  25.0 25.5 %collective-permute-start.2 = (f32[4,4,1,128]{3,2,1,0:T(1,128)S(1)}, f32[4,4,1,128]{3,2,1,0:T(1,128)S(1)}, u32[]{:S(2)}, u32[]{:S(2)}) collective-permute-start(f32[4,4,1,128]{3,2,1,0:T(1,128)S(1)} %get-tuple-element.83), channel_id=1, source_target_pairs={{4,0},{8,4},{12,8},{0,12},{5,1},{9,5},{13,9},{1,13},{6,2},{10,6},{... | collective-permute-start | bytes 24584 | tf_op jit(solution)/shard_map/ppermute | solution.py:25
  26.9 23.6 %collective-permute-start.3 = (f32[4,4,1,128]{3,2,1,0:T(1,128)S(1)}, f32[4,4,1,128]{3,2,1,0:T(1,128)S(1)}, u32[]{:S(2)}, u32[]{:S(2)}) collective-permute-start(f32[4,4,1,128]{3,2,1,0:T(1,128)S(1)} %get-tuple-element.84), channel_id=1, source_target_pairs={{0,4},{4,8},{8,12},{12,0},{1,5},{5,9},{9,13},{13,1},{2,6},{6,10},{... | collective-permute-start | bytes 24584 | tf_op jit(solution)/shard_map/ppermute | solution.py:24
  30.3 20.2 %collective-permute-start.4 = (f32[4,1,8,128]{3,2,1,0:T(8,128)S(1)}, f32[4,1,8,128]{3,2,1,0:T(8,128)S(1)}, u32[]{:S(2)}, u32[]{:S(2)}) collective-permute-start(f32[4,1,8,128]{3,2,1,0:T(8,128)S(1)} %get-tuple-element.85), channel_id=1, source_target_pairs={{16,0},{32,16},{48,32},{64,48},{80,64},{96,80},{112,96},{128,112},... | collective-permute-start | bytes 49160 | tf_op jit(solution)/shard_map/ppermute | solution.py:25
  38.1 12.5 %collective-permute-start.5 = (f32[4,1,8,128]{3,2,1,0:T(8,128)S(1)}, f32[4,1,8,128]{3,2,1,0:T(8,128)S(1)}, u32[]{:S(2)}, u32[]{:S(2)}) collective-permute-start(f32[4,1,8,128]{3,2,1,0:T(8,128)S(1)} %get-tuple-element.86), channel_id=1, source_target_pairs={{0,16},{16,32},{32,48},{48,64},{64,80},{80,96},{96,112},{112,128},... | collective-permute-start | bytes 49160 | tf_op jit(solution)/shard_map/ppermute | solution.py:24
  54.9 18.9 %collective-permute-start.6 = (f32[4,4,8,1]{3,2,1,0:T(8,128)S(1)}, f32[4,4,8,1]{3,2,1,0:T(8,128)S(1)}, u32[]{:S(2)}, u32[]{:S(2)}) collective-permute-start(f32[4,4,8,1]{3,2,1,0:T(8,128)S(1)} %get-tuple-element.69), channel_id=1, source_target_pairs={{1,0},{2,1},{3,2},{0,3},{5,4},{6,5},{7,6},{4,7},{9,8},{10,9},{11,1... | collective-permute-start | bytes 1544 | tf_op jit(solution)/shard_map/ppermute | solution.py:25
  60.4 18.6 %collective-permute-start.8 = (f32[4,4,1,128]{3,2,1,0:T(1,128)S(1)}, f32[4,4,1,128]{3,2,1,0:T(1,128)S(1)}, u32[]{:S(2)}, u32[]{:S(2)}) collective-permute-start(f32[4,4,1,128]{3,2,1,0:T(1,128)S(1)} %get-tuple-element.73), channel_id=1, source_target_pairs={{4,0},{8,4},{12,8},{0,12},{5,1},{9,5},{13,9},{1,13},{6,2},{10,6},{... | collective-permute-start | bytes 24584 | tf_op jit(solution)/shard_map/ppermute | solution.py:25
  65.0 14.1 %collective-permute-start.9 = (f32[4,4,1,128]{3,2,1,0:T(1,128)S(1)}, f32[4,4,1,128]{3,2,1,0:T(1,128)S(1)}, u32[]{:S(2)}, u32[]{:S(2)}) collective-permute-start(f32[4,4,1,128]{3,2,1,0:T(1,128)S(1)} %get-tuple-element.74), channel_id=1, source_target_pairs={{0,4},{4,8},{8,12},{12,0},{1,5},{5,9},{9,13},{13,1},{2,6},{6,10},{... | collective-permute-start | bytes 24584 | tf_op jit(solution)/shard_map/ppermute | solution.py:24
  83.5 18.7 %collective-permute-start.12 = (f32[4,4,8,1]{3,2,1,0:T(8,128)S(1)}, f32[4,4,8,1]{3,2,1,0:T(8,128)S(1)}, u32[]{:S(2)}, u32[]{:S(2)}) collective-permute-start(f32[4,4,8,1]{3,2,1,0:T(8,128)S(1)} %get-tuple-element.59), channel_id=1, source_target_pairs={{1,0},{2,1},{3,2},{0,3},{5,4},{6,5},{7,6},{4,7},{9,8},{10,9},{11,1... | collective-permute-start | bytes 1544 | tf_op jit(solution)/shard_map/ppermute | solution.py:25
  87.8 19.8 %collective-permute-start.14 = (f32[4,4,1,128]{3,2,1,0:T(1,128)S(1)}, f32[4,4,1,128]{3,2,1,0:T(1,128)S(1)}, u32[]{:S(2)}, u32[]{:S(2)}) collective-permute-start(f32[4,4,1,128]{3,2,1,0:T(1,128)S(1)} %get-tuple-element.63), channel_id=1, source_target_pairs={{4,0},{8,4},{12,8},{0,12},{5,1},{9,5},{13,9},{1,13},{6,2},{10,6},{... | collective-permute-start | bytes 24584 | tf_op jit(solution)/shard_map/ppermute | solution.py:25
  92.6 15.0 %collective-permute-start.15 = (f32[4,4,1,128]{3,2,1,0:T(1,128)S(1)}, f32[4,4,1,128]{3,2,1,0:T(1,128)S(1)}, u32[]{:S(2)}, u32[]{:S(2)}) collective-permute-start(f32[4,4,1,128]{3,2,1,0:T(1,128)S(1)} %get-tuple-element.64), channel_id=1, source_target_pairs={{0,4},{4,8},{8,12},{12,0},{1,5},{5,9},{9,13},{13,1},{2,6},{6,10},{... | collective-permute-start | bytes 24584 | tf_op jit(solution)/shard_map/ppermute | solution.py:24
  94.6 13.1 %collective-permute-start.16 = (f32[4,1,8,128]{3,2,1,0:T(8,128)S(1)}, f32[4,1,8,128]{3,2,1,0:T(8,128)S(1)}, u32[]{:S(2)}, u32[]{:S(2)}) collective-permute-start(f32[4,1,8,128]{3,2,1,0:T(8,128)S(1)} %get-tuple-element.65), channel_id=1, source_target_pairs={{16,0},{32,16},{48,32},{64,48},{80,64},{96,80},{112,96},{128,112},... | collective-permute-start | bytes 49160 | tf_op jit(solution)/shard_map/ppermute | solution.py:25
  111.7 18.7 %collective-permute-start.18 = (f32[4,4,8,1]{3,2,1,0:T(8,128)S(1)}, f32[4,4,8,1]{3,2,1,0:T(8,128)S(1)}, u32[]{:S(2)}, u32[]{:S(2)}) collective-permute-start(f32[4,4,8,1]{3,2,1,0:T(8,128)S(1)} %get-tuple-element.49), channel_id=1, source_target_pairs={{1,0},{2,1},{3,2},{0,3},{5,4},{6,5},{7,6},{4,7},{9,8},{10,9},{11,1... | collective-permute-start | bytes 1544 | tf_op jit(solution)/shard_map/ppermute | solution.py:25
  116.0 19.9 %collective-permute-start.20 = (f32[4,4,1,128]{3,2,1,0:T(1,128)S(1)}, f32[4,4,1,128]{3,2,1,0:T(1,128)S(1)}, u32[]{:S(2)}, u32[]{:S(2)}) collective-permute-start(f32[4,4,1,128]{3,2,1,0:T(1,128)S(1)} %get-tuple-element.53), channel_id=1, source_target_pairs={{4,0},{8,4},{12,8},{0,12},{5,1},{9,5},{13,9},{1,13},{6,2},{10,6},{... | collective-permute-start | bytes 24584 | tf_op jit(solution)/shard_map/ppermute | solution.py:25
  120.8 15.0 %collective-permute-start.21 = (f32[4,4,1,128]{3,2,1,0:T(1,128)S(1)}, f32[4,4,1,128]{3,2,1,0:T(1,128)S(1)}, u32[]{:S(2)}, u32[]{:S(2)}) collective-permute-start(f32[4,4,1,128]{3,2,1,0:T(1,128)S(1)} %get-tuple-element.54), channel_id=1, source_target_pairs={{0,4},{4,8},{8,12},{12,0},{1,5},{5,9},{9,13},{13,1},{2,6},{6,10},{... | collective-permute-start | bytes 24584 | tf_op jit(solution)/shard_map/ppermute | solution.py:24
  122.8 13.1 %collective-permute-start.22 = (f32[4,1,8,128]{3,2,1,0:T(8,128)S(1)}, f32[4,1,8,128]{3,2,1,0:T(8,128)S(1)}, u32[]{:S(2)}, u32[]{:S(2)}) collective-permute-start(f32[4,1,8,128]{3,2,1,0:T(8,128)S(1)} %get-tuple-element.55), channel_id=1, source_target_pairs={{16,0},{32,16},{48,32},{64,48},{80,64},{96,80},{112,96},{128,112},... | collective-permute-start | bytes 49160 | tf_op jit(solution)/shard_map/ppermute | solution.py:25
  140.1 24.1 %collective-permute-start.26 = (f32[2,4,1,128]{3,2,1,0:T(1,128)}, f32[2,4,1,128]{3,2,1,0:T(1,128)}, u32[]{:S(2)}, u32[]{:S(2)}) collective-permute-start(f32[2,4,1,128]{3,2,1,0:T(1,128)} %get-tuple-element.129), channel_id=1, source_target_pairs={{4,0},{8,4},{12,8},{0,12},{5,1},{9,5},{13,9},{1,13},{6,2},{10,6},{... | collective-permute-start | bytes 12296 | tf_op jit(solution)/shard_map/ppermute | solution.py:25
  144.9 19.2 %collective-permute-start.27 = (f32[2,4,1,128]{3,2,1,0:T(1,128)}, f32[2,4,1,128]{3,2,1,0:T(1,128)}, u32[]{:S(2)}, u32[]{:S(2)}) collective-permute-start(f32[2,4,1,128]{3,2,1,0:T(1,128)} %get-tuple-element.130), channel_id=1, source_target_pairs={{0,4},{4,8},{8,12},{12,0},{1,5},{5,9},{9,13},{13,1},{2,6},{6,10},{... | collective-permute-start | bytes 12296 | tf_op jit(solution)/shard_map/ppermute | solution.py:24
  147.5 17.7 %collective-permute-start.28 = (f32[2,1,8,128]{3,2,1,0:T(8,128)}, f32[2,1,8,128]{3,2,1,0:T(8,128)}, u32[]{:S(2)}, u32[]{:S(2)}) collective-permute-start(f32[2,1,8,128]{3,2,1,0:T(8,128)} %get-tuple-element.133), channel_id=1, source_target_pairs={{16,0},{32,16},{48,32},{64,48},{80,64},{96,80},{112,96},{128,112},... | collective-permute-start | bytes 24584 | tf_op jit(solution)/shard_map/ppermute | solution.py:25
  181.7 19.4 %collective-permute-start.32 = (f32[2,4,1,128]{3,2,1,0:T(1,128)S(1)}, f32[2,4,1,128]{3,2,1,0:T(1,128)S(1)}, u32[]{:S(2)}, u32[]{:S(2)}) collective-permute-start(f32[2,4,1,128]{3,2,1,0:T(1,128)S(1)} %get-tuple-element.117), channel_id=1, source_target_pairs={{4,0},{8,4},{12,8},{0,12},{5,1},{9,5},{13,9},{1,13},{6,2},{10,6},{... | collective-permute-start | bytes 12296 | tf_op jit(solution)/shard_map/ppermute | solution.py:25
  186.6 14.6 %collective-permute-start.33 = (f32[2,4,1,128]{3,2,1,0:T(1,128)S(1)}, f32[2,4,1,128]{3,2,1,0:T(1,128)S(1)}, u32[]{:S(2)}, u32[]{:S(2)}) collective-permute-start(f32[2,4,1,128]{3,2,1,0:T(1,128)S(1)} %get-tuple-element.118), channel_id=1, source_target_pairs={{0,4},{4,8},{8,12},{12,0},{1,5},{5,9},{9,13},{13,1},{2,6},{6,10},{... | collective-permute-start | bytes 12296 | tf_op jit(solution)/shard_map/ppermute | solution.py:24
  215.9 18.9 %collective-permute-start.38 = (f32[2,4,1,128]{3,2,1,0:T(1,128)S(1)}, f32[2,4,1,128]{3,2,1,0:T(1,128)S(1)}, u32[]{:S(2)}, u32[]{:S(2)}) collective-permute-start(f32[2,4,1,128]{3,2,1,0:T(1,128)S(1)} %get-tuple-element.105), channel_id=1, source_target_pairs={{4,0},{8,4},{12,8},{0,12},{5,1},{9,5},{13,9},{1,13},{6,2},{10,6},{... | collective-permute-start | bytes 12296 | tf_op jit(solution)/shard_map/ppermute | solution.py:25
  220.5 14.4 %collective-permute-start.39 = (f32[2,4,1,128]{3,2,1,0:T(1,128)S(1)}, f32[2,4,1,128]{3,2,1,0:T(1,128)S(1)}, u32[]{:S(2)}, u32[]{:S(2)}) collective-permute-start(f32[2,4,1,128]{3,2,1,0:T(1,128)S(1)} %get-tuple-element.106), channel_id=1, source_target_pairs={{0,4},{4,8},{8,12},{12,0},{1,5},{5,9},{9,13},{13,1},{2,6},{6,10},{... | collective-permute-start | bytes 12296 | tf_op jit(solution)/shard_map/ppermute | solution.py:24
  249.8 18.9 %collective-permute-start.44 = (f32[2,4,1,128]{3,2,1,0:T(1,128)S(1)}, f32[2,4,1,128]{3,2,1,0:T(1,128)S(1)}, u32[]{:S(2)}, u32[]{:S(2)}) collective-permute-start(f32[2,4,1,128]{3,2,1,0:T(1,128)S(1)} %get-tuple-element.93), channel_id=1, source_target_pairs={{4,0},{8,4},{12,8},{0,12},{5,1},{9,5},{13,9},{1,13},{6,2},{10,6},{... | collective-permute-start | bytes 12296 | tf_op jit(solution)/shard_map/ppermute | solution.py:25
  254.4 14.4 %collective-permute-start.45 = (f32[2,4,1,128]{3,2,1,0:T(1,128)S(1)}, f32[2,4,1,128]{3,2,1,0:T(1,128)S(1)}, u32[]{:S(2)}, u32[]{:S(2)}) collective-permute-start(f32[2,4,1,128]{3,2,1,0:T(1,128)S(1)} %get-tuple-element.94), channel_id=1, source_target_pairs={{0,4},{4,8},{8,12},{12,0},{1,5},{5,9},{9,13},{13,1},{2,6},{6,10},{... | collective-permute-start | bytes 12296 | tf_op jit(solution)/shard_map/ppermute | solution.py:24
  (324 other events, 6604.8 us)
